TPU v7x, 256 devices: a whole 4x4x8 slice. The times are simulated.
256 devices in a mesh: dp: 32 (over x, y, core), tensor: 8 (over z).
Axes of the slice: x: 4, y: 4, z: 8, core: 2. Of those that a mesh axis runs over, the one named last changes fastest.
Arguments:
- output_gradient: bfloat16 [8192, 8192], P('dp', 'tensor'), may hold values from -96 to 96
- hidden: bfloat16 [8192, 28672], P('dp', 'tensor'), may hold values from -3 to 3
- adapter_down: bfloat16 [64, 16, 28672], P('dp', None, 'tensor'), may hold values from -0.03125 to 0.03125
- adapter_up: bfloat16 [64, 16, 8192], P('dp', None, 'tensor'), may hold values from -0.0625 to 0.0625
- counts: int32 [64], replicated, may hold values from 32 to 288, as said below
- offsets: int32 [64], replicated, may hold values from 0 to 8160, as said below
- adapter_slot: int32 [64], replicated, may hold values from 0 to 63, as said below
Outputs:
- adapter_hidden_gradient: bfloat16 [8192, 28672], P('dp', 'tensor')
- adapter_down_gradient: float32 [64, 16, 28672], P('dp', None, 'tensor')
- adapter_up_gradient: float32 [64, 16, 8192], P('dp', None, 'tensor')
Inputs may be any that keep to these rules, and one draw needn't show every extreme that they name: counts sum to 8192; the last adapter has exactly 32 tokens; exactly one adapter has 288 tokens, every other fewer. Tokens are grouped by adapter in increasing order: offsets[a] is the sum of counts of the adapters before a. `adapter_slot`: every slot holds exactly one adapter; slot k lies on dp index k // 2, and any 64 // 2 adapters in a row lie on distinct dp indices.
All inputs are finite; a program needn't handle non-finite values.
Results may differ from a plain program's by a relative error of at most 0.0075.
Values may be sent and summed in bfloat16 or wider, within the bound.
No kernel may reach another device: no remote copies, remote signals or barrier semaphores. Data moves between devices by JAX's collectives and lax.ppermute only.
A program may use at most 64 MiB of HBM per device.

v0:
```python
import jax
import jax.numpy as jnp
from jax import lax
from jax.sharding import PartitionSpec as P

adapter_factor = 2.0


def selected_rows(value_entries, shard_portion, member_rows):
    shard_count = shard_portion.shape[0]
    adapter_rank = shard_portion.shape[1]
    flattened_rows = shard_portion.reshape(shard_count * adapter_rank, shard_portion.shape[2])
    rank_scores = lax.dot_general(
        value_entries, flattened_rows, (((1,), (1,)), ((), ())), preferred_element_type=jnp.float32
    )
    selected_entries = member_rows.astype(jnp.float32)
    return jnp.sum(
        rank_scores.reshape(value_entries.shape[0], shard_count, adapter_rank)
        * selected_entries[:, :, None],
        axis=1,
    )


def on_device(output_gradient, hidden, adapter_down, adapter_up, counts, offsets, adapter_slot):
    total_rows = output_gradient.shape[0]
    slots_per_worker = adapter_down.shape[0]
    adapter_rank = adapter_down.shape[1]
    hidden_size_count = hidden.shape[1]
    dp_count = lax.axis_size("dp")
    adapter_list = slots_per_worker * dp_count
    first_token = lax.axis_index("dp") * total_rows
    positions = first_token + lax.broadcasted_iota(jnp.int32, (total_rows, 1), 0)
    inside = (positions >= offsets[None, :]) & (positions < (offsets + counts)[None, :])
    slot_of_row = jnp.sum(jnp.where(inside, adapter_slot[None, :], 0), axis=1)
    columns = lax.broadcasted_iota(jnp.int32, (1, adapter_list), 1)
    member_rows = (slot_of_row[:, None] == columns).astype(jnp.bfloat16)
    up_portion = selected_rows(
        output_gradient, lax.all_gather(adapter_up, "dp", axis=0, tiled=True), member_rows
    )
    up_incoming = lax.psum(up_portion, "tensor").astype(jnp.bfloat16)
    broadcast_up = member_rows[:, :, None] * up_incoming[:, None, :]
    shard_portion = lax.all_gather(adapter_down, "dp", axis=0, tiled=True)
    shard_count = shard_portion.shape[0]
    flattened_rows = shard_portion.reshape(shard_count * adapter_rank, hidden_size_count)
    down_partial = selected_rows(hidden, shard_portion, member_rows)
    broadcast_portion = broadcast_up
    broadcast_portion = broadcast_portion.reshape(total_rows, shard_count * adapter_rank)
    gradient_running = jnp.dot(
        broadcast_portion, flattened_rows, preferred_element_type=jnp.float32
    )
    down_partial, gradient_running = (down_partial, gradient_running)
    down_incoming = lax.psum(down_partial, "tensor").astype(jnp.bfloat16)
    adapter_hidden_gradient = (adapter_factor * gradient_running).astype(jnp.bfloat16)
    broadcast_down = member_rows[:, :, None] * down_incoming[:, None, :]

    def slot_term(spread, value_entries, shard_count):
        broadcast_portion = spread
        broadcast_portion = broadcast_portion.reshape(total_rows, shard_count * adapter_rank)
        matrix_product = lax.dot_general(
            broadcast_portion,
            value_entries,
            (((0,), (0,)), ((), ())),
            preferred_element_type=jnp.float32,
        )
        return matrix_product.reshape(shard_count, adapter_rank, value_entries.shape[1])

    down_reduced = lax.psum_scatter(
        slot_term(broadcast_up, hidden, slots_per_worker * lax.axis_size("dp")).astype(
            jnp.bfloat16
        ),
        "dp",
        scatter_dimension=0,
        tiled=True,
    ).astype(jnp.float32)
    up_reduced = lax.psum_scatter(
        slot_term(broadcast_down, output_gradient, slots_per_worker * lax.axis_size("dp")).astype(
            jnp.bfloat16
        ),
        "dp",
        scatter_dimension=0,
        tiled=True,
    ).astype(jnp.float32)
    slot_grid = adapter_slot[:, None] == columns
    total_slots = jnp.sum(jnp.where(slot_grid, counts[:, None], 0), axis=0)
    scale_entries = adapter_factor / total_slots.astype(jnp.float32)
    owner_scale = lax.dynamic_slice_in_dim(
        scale_entries, lax.axis_index("dp") * slots_per_worker, slots_per_worker, 0
    )
    adapter_down_gradient = down_reduced * owner_scale[:, None, None]
    adapter_up_gradient = up_reduced * owner_scale[:, None, None]
    return (adapter_hidden_gradient, adapter_down_gradient, adapter_up_gradient)


def solution(mesh):
    placed = (
        P("dp", "tensor"),
        P("dp", "tensor"),
        P("dp", None, "tensor"),
        P("dp", None, "tensor"),
        P(),
        P(),
        P(),
    )
    return jax.shard_map(
        on_device,
        mesh=mesh,
        in_specs=placed,
        out_specs=(P("dp", "tensor"), P("dp", None, "tensor"), P("dp", None, "tensor")),
        check_vma=False,
    )
```

profile of v0, /device:TPU:2, one launch (start us, length us, event | category | flops | bytes accessed | tf_op | source)
XLA Modules:
  0.0 353.9 jit_solution(15384436137109650157)
XLA Ops:
  7.2 0.0 copy-start
  7.2 0.0 all-gather.3.cloned.1.call-start
  7.2 0.7 all-gather.3.cloned.1.call-update
  7.9 0.0 all-gather.5.cloned.1.call-start
  8.0 0.7 all-gather.5.cloned.1.call-update
  8.7 0.0 reduce-scatter.5.cloned.1.call-start
  8.7 0.7 add.27
  9.4 0.8 select_reduce_fusion
  10.2 51.6 %all-gather.3.cloned.1.call-done = bf16[64,16,1024]{2,1,0:T(8,128)(2,1)} async-done(((bf16[2,16,1024]{2,1,0:T(8,128)(2,1)}), bf16[64,16,1024]{2,1,0:T(8,128)(2,1)}) %all-gather.3.cloned.1.call-update) | async-done | bytes 2097168 | tf_op jit(solution)/shard_map/all_gather | solution.py:38
  61.8 4.2 %fusion.16 = f32[256,16]{0,1:T(8,128)S(1)} fusion(bf16[64,16,1024]{2,1,0:T(8,128)(2,1)} %all-gather.3.cloned.1.call-done, bf16[256,1024]{1,0:T(8,128)(2,1)} %param.7, f32[256,64]{0,1:T(8,128)S(1)} %get-tuple-element.6), kind=kOutput, calls=%fused_computation.13 | convolution fusion | flops 537391104 | bytes 2703360 | tf_op jit(solution)/shard_map/dot_general | solution.py:13
  66.0 0.0 copy-start.1
  66.0 53.4 %all-gather.5.cloned.1.call-done = bf16[64,16,3584]{2,1,0:T(8,128)(2,1)} async-done(((bf16[2,16,3584]{2,1,0:T(8,128)(2,1)}), bf16[64,16,3584]{2,1,0:T(8,128)(2,1)}) %all-gather.5.cloned.1.call-update) | async-done | bytes 7340048 | tf_op jit(solution)/shard_map/all_gather | solution.py:42
  119.4 0.0 copy-done
  119.4 11.0 %fusion.19 = f32[256,16]{0,1:T(8,128)S(1)} fusion(bf16[64,16,3584]{2,1,0:T(8,128)(2,1)} %all-gather.5.cloned.1.call-done, bf16[256,3584]{1,0:T(8,128)(2,1)S(1)} %copy-done, f32[256,64]{0,1:T(8,128)S(1)} %get-tuple-element.6), kind=kOutput, calls=%fused_computation.14 | convolution fusion | flops 1879568384 | bytes 9256960 | tf_op jit(solution)/shard_map/dot_general | solution.py:13
  130.3 30.3 %all-reduce = (bf16[256,16]{0,1:T(8,128)(2,1)S(1)}, bf16[256,16]{0,1:T(8,128)(2,1)S(1)}) all-reduce(f32[256,16]{0,1:T(8,128)S(1)} %fusion.16, f32[256,16]{0,1:T(8,128)S(1)} %fusion.19), channel_id=1, replica_groups=mesh['dp'=32,'tensor'=8] {'tensor'}, use_global_device_ids=true, to_apply=%region_2.3 | all-reduce | flops 8192 | bytes 49152 | tf_op jit(solution)/shard_map/psum | solution.py:40
  160.6 0.0 copy-done.1
  160.6 2.0 convolution_convert_fusion.1
  162.7 0.0 reduce-scatter.5.cloned.1.call-update
  162.7 0.0 reduce-scatter.3.cloned.1.call-start
  162.8 5.1 %convolution_convert_fusion = bf16[64,16,3584]{2,1,0:T(8,128)(2,1)} fusion(bf16[256,3584]{1,0:T(8,128)(2,1)S(1)} %copy-done, bf16[256,16]{0,1:T(8,128)(2,1)S(1)} %get-tuple-element.3, bf16[256,64]{0,1:T(8,128)(2,1)S(1)} %get-tuple-element.5), kind=kOutput, calls=%fused_computation | convolution fusion | flops 1882980352 | bytes 9216000 | tf_op jit(solution)/shard_map/dot_general | solution.py:59
  167.9 0.0 copy-start.2
  167.9 0.0 copy-start.3
  167.9 0.0 reduce-scatter.3.cloned.1.call-update
  167.9 0.6 copy-done.2
  168.5 0.0 copy-done.3
  168.5 0.1 select_reduce_fusion.1
  168.6 0.1 dynamic_slice.3
  168.7 6.5 %fusion.3 = bf16[256,3584]{1,0:T(8,128)(2,1)} fusion(bf16[64,16,3584]{2,1,0:T(8,128)(2,1)} %all-gather.5.cloned.1.call-done, bf16[256,16]{0,1:T(8,128)(2,1)S(1)} %get-tuple-element.3, bf16[256,64]{0,1:T(8,128)(2,1)S(1)} %get-tuple-element.5), kind=kOutput, calls=%fused_computation.5 | convolution fusion | flops 1881145344 | bytes 9216000 | tf_op jit(solution)/shard_map/dot_general | solution.py:48
  175.2 70.9 %reduce-scatter.5.cloned.1.call-done = bf16[2,16,1024]{2,1,0:T(8,128)(2,1)} async-done(((bf16[64,16,1024]{2,1,0:T(8,128)(2,1)}), bf16[2,16,1024]{2,1,0:T(8,128)(2,1)}) %reduce-scatter.5.cloned.1.call-update) | async-done | bytes 65552 | tf_op jit(solution)/shard_map/reduce_scatter | solution.py:75
  246.1 1.6 convert_multiply_fusion.1
  247.7 97.9 %reduce-scatter.3.cloned.1.call-done = bf16[2,16,3584]{2,1,0:T(8,128)(2,1)} async-done(((bf16[64,16,3584]{2,1,0:T(8,128)(2,1)}), bf16[2,16,3584]{2,1,0:T(8,128)(2,1)}) %reduce-scatter.3.cloned.1.call-update) | async-done | bytes 229392 | tf_op jit(solution)/shard_map/reduce_scatter | solution.py:67
  345.6 1.8 convert_multiply_fusion
  (3 shorter events, 0.0 us)
Async XLA Ops:
  7.2 112.2 %copy-start = (bf16[256,3584]{1,0:T(8,128)(2,1)S(1)}, bf16[256,3584]{1,0:T(8,128)(2,1)}, u32[]{:S(2)}) copy-start(bf16[256,3584]{1,0:T(8,128)(2,1)} %param.8) | copy-start | bytes 5505028
  7.2 54.6 %all-gather.3.cloned.1.call-start = ((), (), s32[]{:S(2)}) async-start(), calls=%async_computation.2 | async-start | bytes 2162688 | tf_op jit(solution)/shard_map/all_gather | solution.py:38
  7.9 111.5 %all-gather.5.cloned.1.call-start = ((), (), s32[]{:S(2)}) async-start(), calls=%async_computation.3 | async-start | bytes 7569408 | tf_op jit(solution)/shard_map/all_gather | solution.py:42
  8.7 237.5 %reduce-scatter.5.cloned.1.call-start = ((), (), s32[]{:S(2)}) async-start(), calls=%async_computation.5 | async-start | bytes 2162688 | tf_op jit(solution)/shard_map/reduce_scatter | solution.py:75
  66.0 94.6 %copy-start.1 = (bf16[256,1024]{1,0:T(8,128)(2,1)S(1)}, bf16[256,1024]{1,0:T(8,128)(2,1)}, u32[]{:S(2)}) copy-start(bf16[256,1024]{1,0:T(8,128)(2,1)} %param.7) | copy-start | bytes 1572868
  162.7 182.9 %reduce-scatter.3.cloned.1.call-start = ((), (), s32[]{:S(2)}) async-start(), calls=%async_computation.4 | async-start | bytes 7569408 | tf_op jit(solution)/shard_map/reduce_scatter | solution.py:67
  167.9 0.7 copy-start.2
  167.9 0.7 copy-start.3
Sparse Core Ops, SparseCore 0:
  10.5 51.1 all-gather.2
  64.3 55.0 all-gather.4
  162.8 83.2 reduce-scatter.4
  250.0 95.5 reduce-scatter.2
where the time goes:
time: 354 us
  waiting for transfers between devices  275 us (78%)
  blocking collectives  30.3 us (9%)
  matrix products  28.8 us (8%)
  between operations  13.8 us (4%)
  other arithmetic  4.95 us (1%)
    reduce_scatter x1, waiting for transfers between devices, on_device(): lax.psum_scatter(slot_term(broadcast_up, hidden, slots_per_worker * lax.a...  97.9 us
    reduce_scatter x1, waiting for transfers between devices, on_device(): lax.psum_scatter(slot_term(broadcast_down, output_gradient, slots_per_wor...  70.9 us
    all_gather x1, waiting for transfers between devices, on_device(): shard_portion = lax.all_gather(adapter_down, 'dp', axis=0, tiled=True)  53.4 us
    all_gather x1, waiting for transfers between devices, on_device(): lax.all_gather(adapter_up, 'dp', axis=0, tiled=True)  51.6 us
    psum x1, blocking collectives, on_device(): up_incoming = lax.psum(up_portion, 'tensor').astype(jnp.bfloat16)  30.3 us
    dot_general x2, matrix products, selected_rows(): lax.dot_general(value_entries, flattened_rows, (((1,), (1,)), ((), ())),...  15.2 us
    dot_general x2, matrix products, slot_term(): lax.dot_general(broadcast_portion, value_entries, (((0,), (0,)), ((), ())...  7.15 us
  transfers between devices with their start and end apart: 4, of which 4 were waited for; matrix products, arithmetic and copies ran while one was open for 5% of the time, Pallas kernels for 0%

commit v1 on v0

--- a/solution.py
+++ b/solution.py
@@ -4,6 +4,11 @@
 from jax.sharding import PartitionSpec as P
 
 adapter_factor = 2.0
+
+
+def summed_here(shard, axis):
+    parts = lax.all_gather(shard, axis)
+    return jnp.sum(parts, axis=0)
 
 
 def selected_rows(value_entries, shard_portion, member_rows):
@@ -37,7 +42,7 @@
     up_portion = selected_rows(
         output_gradient, lax.all_gather(adapter_up, "dp", axis=0, tiled=True), member_rows
     )
-    up_incoming = lax.psum(up_portion, "tensor").astype(jnp.bfloat16)
+    up_incoming = summed_here(up_portion, "tensor").astype(jnp.bfloat16)
     broadcast_up = member_rows[:, :, None] * up_incoming[:, None, :]
     shard_portion = lax.all_gather(adapter_down, "dp", axis=0, tiled=True)
     shard_count = shard_portion.shape[0]

time: 354 us -> 317 us (0.90)
  waiting for transfers between devices: 275 us -> 212 us
  blocking collectives: 30.3 us -> 56.2 us
    reduce_scatter x1, waiting for transfers between devices: 97.9 us -> 49.9 us  [on_device(): lax.psum_scatter(slot_term(broadcast_up, hidden, slots_per_worker * lax.a...]
    all_gather x1, waiting for transfers between devices: 53.4 us -> 21.3 us  [on_device(): shard_portion = lax.all_gather(adapter_down, 'dp', axis=0, tiled=True)]
    all_gather x0 -> x1, blocking collectives: none -> 26 us  [summed_here(): parts = lax.all_gather(shard, axis)]
    reduce_scatter x1, waiting for transfers between devices: 70.9 us -> 87.8 us  [on_device(): lax.psum_scatter(slot_term(broadcast_down, output_gradient, slots_per_wor...]
  transfers between devices with their start and end apart: 4 -> 4, of which waited for: 4 -> 4; matrix products, arithmetic and copies ran while one was open for 5% -> 10% of each run, Pallas kernels for 0% -> 0%
where the time goes in v1:
time: 317 us
  waiting for transfers between devices  212 us (67%)
  blocking collectives  56.2 us (18%)
  matrix products  28.8 us (9%)
  between operations  13.8 us (4%)
  other arithmetic  4.99 us (2%)
    reduce_scatter x1, waiting for transfers between devices, on_device(): lax.psum_scatter(slot_term(broadcast_down, output_gradient, slots_per_wor...  87.8 us
    all_gather x1, waiting for transfers between devices, on_device(): lax.all_gather(adapter_up, 'dp', axis=0, tiled=True)  51.6 us
    reduce_scatter x1, waiting for transfers between devices, on_device(): lax.psum_scatter(slot_term(broadcast_up, hidden, slots_per_worker * lax.a...  49.9 us
    psum x1, blocking collectives, on_device(): down_incoming = lax.psum(down_partial, 'tensor').astype(jnp.bfloat16)  30.2 us
    all_gather x1, blocking collectives, summed_here(): parts = lax.all_gather(shard, axis)  26 us
    all_gather x1, waiting for transfers between devices, on_device(): shard_portion = lax.all_gather(adapter_down, 'dp', axis=0, tiled=True)  21.3 us
    dot_general x2, matrix products, selected_rows(): lax.dot_general(value_entries, flattened_rows, (((1,), (1,)), ((), ())),...  15.2 us
    dot_general x2, matrix products, slot_term(): lax.dot_general(broadcast_portion, value_entries, (((0,), (0,)), ((), ())...  7.15 us
  transfers between devices with their start and end apart: 4, of which 4 were waited for; matrix products, arithmetic and copies ran while one was open for 10% of the time, Pallas kernels for 0%

profile of v1, /device:TPU:2, one launch (start us, length us, event | category | flops | bytes accessed | tf_op | source)
XLA Modules:
  0.0 316.7 jit_solution(1351142453008852418)
XLA Ops:
  7.2 0.0 copy-start
  7.2 0.0 all-gather.4.cloned.1.call-start
  7.2 0.7 all-gather.4.cloned.1.call-update
  7.9 0.0 all-gather.6.cloned.1.call-start
  8.0 0.7 all-gather.6.cloned.1.call-update
  8.7 0.0 reduce-scatter.3.cloned.1.call-start
  8.7 0.7 add.25
  9.4 0.8 select_reduce_fusion
  10.2 51.6 %all-gather.4.cloned.1.call-done = bf16[64,16,1024]{2,1,0:T(8,128)(2,1)} async-done(((bf16[2,16,1024]{2,1,0:T(8,128)(2,1)}), bf16[64,16,1024]{2,1,0:T(8,128)(2,1)}) %all-gather.4.cloned.1.call-update) | async-done | bytes 2097168 | tf_op jit(solution)/shard_map/all_gather | solution.py:43
  61.8 4.2 %fusion.16 = f32[256,16]{0,1:T(8,128)S(1)} fusion(bf16[64,16,1024]{2,1,0:T(8,128)(2,1)} %all-gather.4.cloned.1.call-done, bf16[256,1024]{1,0:T(8,128)(2,1)} %param.7, f32[256,64]{0,1:T(8,128)S(1)} %get-tuple-element.4), kind=kOutput, calls=%fused_computation.13 | convolution fusion | flops 537391104 | bytes 2703360 | tf_op jit(solution)/shard_map/dot_general | solution.py:18
  66.0 26.0 %all-gather = f32[2048,16]{0,1:T(8,128)S(1)} all-gather(f32[256,16]{0,1:T(8,128)S(1)} %fusion.16), channel_id=2, replica_groups=mesh['dp'=32,'tensor'=8] {'tensor'}, dimensions={0}, use_global_device_ids=true | all-gather | bytes 147456 | tf_op jit(solution)/shard_map/all_gather | solution.py:10
  92.1 0.0 copy-done
  92.1 5.1 %convolution_convert_fusion = bf16[64,16,3584]{2,1,0:T(8,128)(2,1)} fusion(bf16[256,3584]{1,0:T(8,128)(2,1)S(1)} %copy-done, bf16[256,16]{0,1:T(8,128)(2,1)S(1)} %bitcast_reduce_fusion, bf16[256,64]{0,1:T(8,128)(2,1)S(1)} %get-tuple-element.3), kind=kOutput, calls=%fused_computation | convolution fusion | flops 1882980352 | bytes 9216000 | tf_op jit(solution)/shard_map/dot_general | solution.py:64
  97.2 0.0 copy-start.2
  97.2 0.0 copy-start.3
  97.2 0.0 reduce-scatter.3.cloned.1.call-update
  97.3 0.2 reduce-scatter.5.cloned.1.call-start
  97.5 0.4 copy-done.2
  97.9 0.0 copy-done.3
  97.9 0.1 select_reduce_fusion.1
  98.0 0.1 dynamic_slice.3
  98.1 21.3 %all-gather.6.cloned.1.call-done = bf16[64,16,3584]{2,1,0:T(8,128)(2,1)} async-done(((bf16[2,16,3584]{2,1,0:T(8,128)(2,1)}), bf16[64,16,3584]{2,1,0:T(8,128)(2,1)}) %all-gather.6.cloned.1.call-update) | async-done | bytes 7340048 | tf_op jit(solution)/shard_map/all_gather | solution.py:47
  119.4 11.0 %fusion.19 = f32[256,16]{0,1:T(8,128)S(1)} fusion(bf16[64,16,3584]{2,1,0:T(8,128)(2,1)} %all-gather.6.cloned.1.call-done, bf16[256,3584]{1,0:T(8,128)(2,1)S(1)} %copy-done, f32[256,64]{0,1:T(8,128)S(1)} %get-tuple-element.4), kind=kOutput, calls=%fused_computation.14 | convolution fusion | flops 1879568384 | bytes 9256960 | tf_op jit(solution)/shard_map/dot_general | solution.py:18
  130.4 30.2 %psum.7 = bf16[256,16]{0,1:T(8,128)(2,1)S(1)} all-reduce(f32[256,16]{0,1:T(8,128)S(1)} %fusion.19), channel_id=1, replica_groups=mesh['dp'=32,'tensor'=8] {'tensor'}, use_global_device_ids=true, to_apply=%region_6.7 | all-reduce | flops 4096 | bytes 24576 | tf_op jit(solution)/shard_map/psum | solution.py:57
  160.6 0.0 copy-done.1
  160.6 2.0 convolution_convert_fusion.1
  162.6 0.0 reduce-scatter.5.cloned.1.call-update
  162.6 6.4 %fusion.3 = bf16[256,3584]{1,0:T(8,128)(2,1)} fusion(bf16[64,16,3584]{2,1,0:T(8,128)(2,1)} %all-gather.6.cloned.1.call-done, bf16[256,16]{0,1:T(8,128)(2,1)S(1)} %bitcast_reduce_fusion, bf16[256,64]{0,1:T(8,128)(2,1)S(1)} %get-tuple-element.3), kind=kOutput, calls=%fused_computation.5 | convolution fusion | flops 1881145344 | bytes 9216000 | tf_op jit(solution)/shard_map/dot_general | solution.py:53
  169.1 49.9 %reduce-scatter.3.cloned.1.call-done = bf16[2,16,3584]{2,1,0:T(8,128)(2,1)} async-done(((bf16[64,16,3584]{2,1,0:T(8,128)(2,1)}), bf16[2,16,3584]{2,1,0:T(8,128)(2,1)}) %reduce-scatter.3.cloned.1.call-update) | async-done | bytes 229392 | tf_op jit(solution)/shard_map/reduce_scatter | solution.py:72
  219.0 1.8 convert_multiply_fusion
  220.8 87.8 %reduce-scatter.5.cloned.1.call-done = bf16[2,16,1024]{2,1,0:T(8,128)(2,1)} async-done(((bf16[64,16,1024]{2,1,0:T(8,128)(2,1)}), bf16[2,16,1024]{2,1,0:T(8,128)(2,1)}) %reduce-scatter.5.cloned.1.call-update) | async-done | bytes 65552 | tf_op jit(solution)/shard_map/reduce_scatter | solution.py:80
  308.6 1.6 convert_multiply_fusion.1
  (6 shorter events, 0.1 us)
Async XLA Ops:
  7.2 84.9 %copy-start = (bf16[256,3584]{1,0:T(8,128)(2,1)S(1)}, bf16[256,3584]{1,0:T(8,128)(2,1)}, u32[]{:S(2)}) copy-start(bf16[256,3584]{1,0:T(8,128)(2,1)} %param.8) | copy-start | bytes 5505028
  7.2 54.6 %all-gather.4.cloned.1.call-start = ((), (), s32[]{:S(2)}) async-start(), calls=%async_computation.2 | async-start | bytes 2162688 | tf_op jit(solution)/shard_map/all_gather | solution.py:43
  7.9 111.5 %all-gather.6.cloned.1.call-start = ((), (), s32[]{:S(2)}) async-start(), calls=%async_computation.3 | async-start | bytes 7569408 | tf_op jit(solution)/shard_map/all_gather | solution.py:47
  8.7 210.3 %reduce-scatter.3.cloned.1.call-start = ((), (), s32[]{:S(2)}) async-start(), calls=%async_computation.4 | async-start | bytes 7569408 | tf_op jit(solution)/shard_map/reduce_scatter | solution.py:72
  97.2 0.7 copy-start.2
  97.2 0.7 copy-start.3
  97.3 211.4 %reduce-scatter.5.cloned.1.call-start = ((), (), s32[]{:S(2)}) async-start(), calls=%async_computation.5 | async-start | bytes 2162688 | tf_op jit(solution)/shard_map/reduce_scatter | solution.py:80
  98.1 62.5 %copy-start.1 = (bf16[256,1024]{1,0:T(8,128)(2,1)S(1)}, bf16[256,1024]{1,0:T(8,128)(2,1)}, u32[]{:S(2)}) copy-start(bf16[256,1024]{1,0:T(8,128)(2,1)} %param.7) | copy-start | bytes 1572868
Sparse Core Ops, SparseCore 0:
  10.5 51.1 all-gather.3
  64.3 55.0 all-gather.5
  123.4 95.4 reduce-scatter.2
  222.7 85.9 reduce-scatter.4
